TPU v7x, 32 devices: a whole 2x2x4 slice. The times are simulated.
32 devices in a mesh: fsdp: 2 (over x), ctx: 4 (over z), tp: 4 (over y, core).
Axes of the slice: x: 2, y: 2, z: 4, core: 2. Of those that a mesh axis runs over, the one named last changes fastest.
Arguments:
- tokens: bfloat16 [8192, 1024], P(('fsdp', 'ctx')), may hold values from -6 to 6
- w_qkv: bfloat16 [3, 1024, 1024], P(None, 'fsdp', 'tp'), may hold values from -0.25 to 0.25
- w_out: bfloat16 [1024, 1024], P('tp', 'fsdp'), may hold values from -0.75 to 0.75
- w_up: bfloat16 [1024, 4096], P('fsdp', 'tp'), may hold values from -0.1875 to 0.1875
- w_down: bfloat16 [4096, 1024], P('tp', 'fsdp'), may hold values from -0.09375 to 0.09375
- gains: bfloat16 [2, 1024], P(None, 'fsdp'), may hold values from 0.5 to 1.5
- shifts: bfloat16 [2, 1024], P(None, 'fsdp'), may hold values from -3 to 3
- lengths: int32 [2, 3], P('fsdp'), may hold values from 256 to 2048, as said below
- out_grad: bfloat16 [8192, 1024], P(('fsdp', 'ctx')), may hold values from -6 to 6
Outputs:
- out: bfloat16 [8192, 1024], P(('fsdp', 'ctx'))
- input_grad: bfloat16 [8192, 1024], P(('fsdp', 'ctx'))
- grad_qkv: float32 [3, 1024, 1024], P(None, 'fsdp', 'tp')
- grad_out: float32 [1024, 1024], P('tp', 'fsdp')
- grad_up: float32 [1024, 4096], P('fsdp', 'tp')
- grad_down: float32 [4096, 1024], P('tp', 'fsdp')
- grad_gains: float32 [2, 1024], P(None, 'fsdp')
- grad_shifts: float32 [2, 1024], P(None, 'fsdp')
Inputs may be any that keep to these rules, and one draw needn't show every extreme that they name: `lengths`: in each row one sequence has exactly 2048 tokens and the others 2048 // 8 to 1024; sequences lie end to end from the pack's first slot, and the slots after them up to 4096 are padding.
All inputs are finite; a program needn't handle non-finite values.
Results may differ from a plain program's by a relative error of at most 0.014.
The roundings to bfloat16 on the way count: a program that leaves them out, or rounds other values in their place, can miss the bound.
Values may be sent and summed in bfloat16 or wider, within the bound.
No kernel may reach another device: no remote copies, remote signals or barrier semaphores. Data moves between devices by JAX's collectives and lax.ppermute only.
A program may use at most 192 MiB of HBM per device.

v0:
```python
import math
import jax
import jax.numpy as jnp
from jax import lax
from jax.sharding import PartitionSpec as P

HEAD_DIM = 64
SEQS = 3
norm_eps = 1e-12
masked_low = -1e30


def layer_norm(rows, gain, shift):
    centre = rows - jnp.mean(rows, axis=-1, keepdims=True)
    spread = jnp.mean(centre * centre, axis=-1, keepdims=True)
    return centre * lax.rsqrt(spread + norm_eps) * gain + shift


def exact_gelu(values):
    return jax.nn.gelu(values, approximate=False)


def contract_rows(left, right):
    return lax.dot_general(
        left, right, (((0,), (0,)), ((), ())), preferred_element_type=jnp.float32
    )


def contract_cols(left, right):
    return lax.dot_general(
        left, right, (((1,), (1,)), ((), ())), preferred_element_type=jnp.float32
    )


def tp_total(terms):
    return lax.psum(terms, "tp")


def segment_of(lengths_row, total):
    seq_ends = jnp.cumsum(lengths_row)
    positions = jnp.arange(total, dtype=jnp.int32)
    return jnp.sum((positions[:, None] >= seq_ends[None, :]).astype(jnp.int32), axis=1)


def score_block(query_block, seg_block, key_heads, segments):
    raw_scores = jnp.einsum(
        "qhd,khd->hqk", query_block, key_heads, preferred_element_type=jnp.float32
    )
    allowed = (seg_block[:, None] == segments[None, :]) & (segments[None, :] < SEQS)
    return (raw_scores * (1.0 / math.sqrt(HEAD_DIM)), allowed)


def attend_forward(query_heads, seg_mine, key_heads, value_heads, segments):

    def one_block(inputs):
        query_block, seg_block = inputs
        scores, allowed = score_block(query_block, seg_block, key_heads, segments)
        has_key = jnp.any(allowed, axis=1)
        masked = jnp.where(allowed[None], scores, masked_low)
        row_max = jnp.where(has_key[None, :, None], jnp.max(masked, axis=2, keepdims=True), 0.0)
        exp_terms = jnp.where(allowed[None], jnp.exp(masked - row_max), 0.0)
        denominator = (
            jnp.sum(exp_terms, axis=2, keepdims=True)
            + (1.0 - has_key.astype(jnp.float32))[None, :, None]
        )
        attn_probs = (exp_terms / denominator).astype(jnp.bfloat16)
        context = jnp.einsum(
            "hqk,khd->qhd", attn_probs, value_heads, preferred_element_type=jnp.float32
        )
        log_total = row_max[:, :, 0] + jnp.log(denominator[:, :, 0])
        return (context.astype(jnp.bfloat16), log_total)

    return lax.map(one_block, (query_heads, seg_mine))


def attend_backward(
    query_heads, seg_mine, grad_heads, log_totals, key_heads, value_heads, segments
):
    score_scale = 1.0 / math.sqrt(HEAD_DIM)
    zero_keys = jnp.zeros(key_heads.shape, jnp.float32)

    def one_block(carry, inputs):
        key_grad, value_grad = carry
        query_block, seg_block, grad_block, log_block = inputs
        scores, allowed = score_block(query_block, seg_block, key_heads, segments)
        attn_probs = jnp.where(allowed[None], jnp.exp(scores - log_block[:, :, None]), 0.0)
        probs_low = attn_probs.astype(jnp.bfloat16)
        grad_probs = jnp.einsum(
            "qhd,khd->hqk", grad_block, value_heads, preferred_element_type=jnp.float32
        )
        row_delta = jnp.sum(attn_probs * grad_probs, axis=2, keepdims=True)
        grad_scores = (attn_probs * (grad_probs - row_delta) * score_scale).astype(jnp.bfloat16)
        query_grad = jnp.einsum(
            "hqk,khd->qhd", grad_scores, key_heads, preferred_element_type=jnp.float32
        )
        key_grad = key_grad + jnp.einsum(
            "hqk,qhd->khd", grad_scores, query_block, preferred_element_type=jnp.float32
        )
        value_grad = value_grad + jnp.einsum(
            "hqk,qhd->khd", probs_low, grad_block, preferred_element_type=jnp.float32
        )
        return ((key_grad, value_grad), query_grad)

    return lax.scan(
        one_block, (zero_keys, zero_keys), (query_heads, seg_mine, grad_heads, log_totals)
    )


def body(tokens, w_qkv, w_out, w_up, w_down, gains, shifts, lengths, out_grad):
    full_qkv, full_out, full_up, full_down, full_gains, full_shifts = (
        lax.all_gather(w_qkv, "fsdp", axis=1, tiled=True),
        lax.all_gather(w_out, "fsdp", axis=1, tiled=True),
        lax.all_gather(w_up, "fsdp", axis=0, tiled=True),
        lax.all_gather(w_down, "fsdp", axis=1, tiled=True),
        lax.all_gather(gains, "fsdp", axis=1, tiled=True),
        lax.all_gather(shifts, "fsdp", axis=1, tiled=True),
    )
    tok_rows = tokens.shape[0]
    local_width = full_qkv.shape[2]
    local_heads = local_width // HEAD_DIM
    block_rows = min(512, tok_rows)
    block_count = tok_rows // block_rows
    pack_rows = tok_rows * lax.axis_size("ctx")
    segments = segment_of(lengths[0], pack_rows)
    seg_mine = lax.dynamic_slice_in_dim(
        segments, lax.axis_index("ctx") * tok_rows, tok_rows
    ).reshape(block_count, block_rows)
    residual_in = tokens.astype(jnp.float32)
    projected = jnp.einsum(
        "td,sdc->stc", tokens, full_qkv, preferred_element_type=jnp.float32
    ).astype(jnp.bfloat16)
    key_rows, value_rows = (
        lax.all_gather(projected[1], "ctx", axis=0, tiled=True),
        lax.all_gather(projected[2], "ctx", axis=0, tiled=True),
    )
    key_heads = key_rows.reshape(pack_rows, local_heads, HEAD_DIM)
    value_heads = value_rows.reshape(pack_rows, local_heads, HEAD_DIM)
    query_heads = projected[0].reshape(block_count, block_rows, local_heads, HEAD_DIM)
    context_blocks, log_totals = attend_forward(
        query_heads, seg_mine, key_heads, value_heads, segments
    )
    context = context_blocks.reshape(tok_rows, local_width)
    attn_terms = jnp.dot(context, full_out, preferred_element_type=jnp.float32)
    resid_rows = residual_in + tp_total(attn_terms)
    grad_rows = out_grad.astype(jnp.float32)
    gain_full = full_gains.astype(jnp.float32)
    shift_full = full_shifts.astype(jnp.float32)
    hidden, norm_first = jax.vjp(layer_norm, resid_rows, gain_full[0], shift_full[0])
    hidden_part = hidden.astype(jnp.bfloat16)
    pre_act = jnp.dot(hidden_part, full_up, preferred_element_type=jnp.float32)
    activated, gelu_back = jax.vjp(exact_gelu, pre_act)
    act_low = activated.astype(jnp.bfloat16)
    ffn_terms = jnp.dot(act_low, full_down, preferred_element_type=jnp.float32)
    ffn_rows = tp_total(ffn_terms)
    result, norm_second = jax.vjp(layer_norm, hidden + ffn_rows, gain_full[1], shift_full[1])
    grad_mid, gain_second, shift_second = norm_second(grad_rows)
    mid_part = grad_mid.astype(jnp.bfloat16)
    result_part = result.astype(jnp.bfloat16)
    back_qkv, back_out, back_up, back_down = (
        lax.all_gather(w_qkv, "fsdp", axis=1, tiled=True),
        lax.all_gather(w_out, "fsdp", axis=1, tiled=True),
        lax.all_gather(w_up, "fsdp", axis=0, tiled=True),
        lax.all_gather(w_down, "fsdp", axis=1, tiled=True),
    )
    down_grad = contract_rows(act_low, mid_part)
    act_grad = contract_cols(mid_part, back_down)
    (pre_grad,) = gelu_back(act_grad)
    pre_low = pre_grad.astype(jnp.bfloat16)
    up_grad = contract_rows(hidden_part, pre_low)
    hidden_terms = contract_cols(pre_low, back_up)
    hidden_grad = grad_mid + tp_total(hidden_terms)
    resid_grad, gain_first, shift_first = norm_first(hidden_grad)
    attn_part = resid_grad.astype(jnp.bfloat16)
    out_proj_grad = contract_rows(context, attn_part)
    context_grad = contract_cols(attn_part, back_out).astype(jnp.bfloat16)
    grad_heads = context_grad.reshape(block_count, block_rows, local_heads, HEAD_DIM)
    (key_grad, value_grad), query_grad = attend_backward(
        query_heads, seg_mine, grad_heads, log_totals, key_heads, value_heads, segments
    )
    key_mine, value_mine = (
        lax.psum_scatter(
            key_grad.reshape(pack_rows, local_width), "ctx", scatter_dimension=0, tiled=True
        ),
        lax.psum_scatter(
            value_grad.reshape(pack_rows, local_width), "ctx", scatter_dimension=0, tiled=True
        ),
    )
    proj_grad = jnp.stack(
        [
            query_grad.reshape(tok_rows, local_width).astype(jnp.bfloat16),
            key_mine.astype(jnp.bfloat16),
            value_mine.astype(jnp.bfloat16),
        ]
    )
    qkv_grad = jnp.einsum("td,stc->sdc", tokens, proj_grad, preferred_element_type=jnp.float32)
    input_part = jnp.einsum("stc,sdc->td", proj_grad, back_qkv, preferred_element_type=jnp.float32)
    input_grad = (resid_grad + tp_total(input_part)).astype(jnp.bfloat16)
    gain_grad = jnp.stack([gain_first, gain_second])
    shift_grad = jnp.stack([shift_first, shift_second])
    qkv_grad, out_proj_grad, up_grad, down_grad, gain_grad, shift_grad = (
        lax.psum_scatter(qkv_grad, "fsdp", scatter_dimension=1, tiled=True),
        lax.psum_scatter(out_proj_grad, "fsdp", scatter_dimension=1, tiled=True),
        lax.psum_scatter(up_grad, "fsdp", scatter_dimension=0, tiled=True),
        lax.psum_scatter(down_grad, "fsdp", scatter_dimension=1, tiled=True),
        lax.psum_scatter(gain_grad, "fsdp", scatter_dimension=1, tiled=True),
        lax.psum_scatter(shift_grad, "fsdp", scatter_dimension=1, tiled=True),
    )
    qkv_grad, out_proj_grad, up_grad, down_grad, gain_grad, shift_grad = lax.psum(
        (qkv_grad, out_proj_grad, up_grad, down_grad, gain_grad, shift_grad), "ctx"
    )
    return (
        result_part,
        input_grad,
        qkv_grad,
        out_proj_grad,
        up_grad,
        down_grad,
        gain_grad,
        shift_grad,
    )


def solution(mesh):
    return jax.shard_map(
        body,
        mesh=mesh,
        in_specs=(
            P(("fsdp", "ctx"), None),
            P(None, "fsdp", "tp"),
            P("tp", "fsdp"),
            P("fsdp", "tp"),
            P("tp", "fsdp"),
            P(None, "fsdp"),
            P(None, "fsdp"),
            P("fsdp", None),
            P(("fsdp", "ctx"), None),
        ),
        out_specs=(
            P(("fsdp", "ctx"), None),
            P(("fsdp", "ctx"), None),
            P(None, "fsdp", "tp"),
            P("tp", "fsdp"),
            P("fsdp", "tp"),
            P("tp", "fsdp"),
            P(None, "fsdp"),
            P(None, "fsdp"),
        ),
        check_vma=False,
    )
```

profile of v0, /device:TPU:0, one launch (start us, length us, event | category | flops | bytes accessed | tf_op | source)
XLA Modules:
  0.0 1667.1 jit_solution(5852999273512513464)
XLA Ops:
  9.6 30.5 %all-gather.8.cloned.1.call-done = bf16[3,1024,256]{1,2,0:T(8,128)(2,1)} async-done(((bf16[3,512,256]{1,2,0:T(8,128)(2,1)}), bf16[3,1024,256]{1,2,0:T(8,128)(2,1)}) %all-gather.8.cloned.1.call-update) | async-done | bytes 1572880 | tf_op jit(solution)/shard_map/all_gather | solution.py:111
  40.1 3.9 fusion.111
  46.3 9.0 all_gather.31
  55.7 35.5 %all-gather.14.cloned.1.call-done = bf16[1,4096,256]{1,2,0:T(8,128)(2,1)} async-done(((bf16[1,1024,256]{1,2,0:T(8,128)(2,1)}), bf16[1,4096,256]{1,2,0:T(8,128)(2,1)}) %all-gather.14.cloned.1.call-update) | async-done | bytes 2097168 | tf_op jit(solution)/shard_map/all_gather | solution.py:133
  91.2 46.9 %all-gather.16.cloned.1.call-done = bf16[1,4096,256]{1,2,0:T(8,128)(2,1)} async-done(((bf16[1,1024,256]{1,2,0:T(8,128)(2,1)}), bf16[1,4096,256]{1,2,0:T(8,128)(2,1)}) %all-gather.16.cloned.1.call-update) | async-done | bytes 2097168 | tf_op jit(solution)/shard_map/all_gather | solution.py:134
  138.0 99.9 %while.27 = (s32[]{:T(128)}, bf16[2,512,4,64]{1,3,2,0:T(8,128)(2,1)}, f32[2,4,512]{2,1,0:T(4,128)S(1)}, s32[2,512]{1,0:T(2,128)S(1)}, s32[4096]{0:T(1024)S(1)}, ...) while((s32[]{:T(128)}, ...), condition=%wide.region_6.7_spmd, body=%wide.region_2.6_spmd.sunk | while | flops 2271357440 | bytes 113924704 | solution.py:73
  140.3 15.8 fusion.181
  156.1 15.6 fusion.182
  171.8 16.2 fusion.183
  190.3 15.8 fusion.181
  206.1 15.6 fusion.182
  221.7 16.2 fusion.183
  240.4 2.7 fusion.134
  244.4 4.3 all_gather.32
  248.7 4.6 all_gather.33
  253.3 74.2 %all-reduce.8.cloned.1.call-done = f32[1024,1024]{1,0:T(8,128)} async-done(((f32[1024,1024]{1,0:T(8,128)}), f32[1024,1024]{1,0:T(8,128)}) %all-reduce.8.cloned.1.call-update) | async-done | bytes 4194320 | tf_op jit(solution)/shard_map/psum | solution.py:36
  327.5 2.7 fusion.130
  332.7 29.5 %all-gather.10.cloned.1.call-done = bf16[1024,1024]{1,0:T(8,128)(2,1)} async-done(((bf16[512,1024]{1,0:T(8,128)(2,1)}), bf16[1024,1024]{1,0:T(8,128)(2,1)}) %all-gather.10.cloned.1.call-update) | async-done | bytes 2097168 | tf_op jit(solution)/shard_map/all_gather | solution.py:113
  362.2 15.5 multiply_convert_fusion.1
  377.7 19.1 %all-gather.12.cloned.1.call-done = bf16[1024,1024]{1,0:T(8,128)(2,1)} async-done(((bf16[1024,512]{1,0:T(8,128)(2,1)}), bf16[1024,1024]{1,0:T(8,128)(2,1)}) %all-gather.12.cloned.1.call-update) | async-done | bytes 2097168 | tf_op jit(solution)/shard_map/all_gather | solution.py:114
  396.9 6.5 fusion.135
  403.8 85.2 %all-reduce.10.cloned.1.call-done = f32[1024,1024]{1,0:T(8,128)} async-done(((f32[1024,1024]{1,0:T(8,128)}), f32[1024,1024]{1,0:T(8,128)}) %all-reduce.10.cloned.1.call-update) | async-done | bytes 4194320 | tf_op jit(solution)/shard_map/psum | solution.py:36
  489.0 4.2 fusion.127
  497.5 3.2 fusion.126
  500.6 3.1 copy-done.39
  503.7 3.9 add_convert_fusion.1
  509.0 4.3 fusion.136
  513.4 85.7 %all-reduce.12.cloned.1.call-done = f32[1024,1024]{1,0:T(8,128)} async-done(((f32[1024,1024]{1,0:T(8,128)}), f32[1024,1024]{1,0:T(8,128)}) %all-reduce.12.cloned.1.call-update) | async-done | bytes 4194320 | tf_op jit(solution)/shard_map/psum | solution.py:36
  599.1 6.4 multiply_reduce_fusion.1
  610.8 2.8 reshape.357
  615.2 341.7 %while.28 = (s32[]{:T(128)}, f32[4096,4,64]{0,2,1:T(8,128)}, f32[4096,4,64]{0,2,1:T(8,128)}, bf16[2,512,4,64]{1,3,2,0:T(8,128)(2,1)}, bf16[2,512,4,64]{1,3,2,0:T...) while((s32[]{:T(128)}, f32[4096,4,64]{0,2,1:T(8,128)}, ...), condition=%wide.region_20.21_spmd.clone, body=%wide.region_18.20_spmd.clone.sunk | while | flops 5595217920 | bytes 414817440 | solution.py:104
  615.4 2.8 compare_and_fusion.3
  618.2 13.1 fusion.196
  631.3 13.1 fusion.195
  644.4 63.5 %fusion.197 = f32[4096,4,64]{0,2,1:T(8,128)} fusion(f32[4,512,4096]{2,1,0:T(8,128)} %fusion.195, f32[4,512,4096]{2,1,0:T(8,128)} %fusion.196, f32[4,512]{1,0:T(4,128)S(1)} %dynamic-slice_bitcast_fusion.2, pred[512,4096]{1,0:T(8,128)(4,1)} %compare_and_fusion.3, f32[4096,4,64]{0,2,1:T(8,128)} %get-tuple-element.498, pred[]{:T(512)S(6)} %compare.3, ...), kind=kOutput, calls=%fused_computation.48.clone.1 | convolution fusion | flops 1168119808 | bytes 147079680 | tf_op jit(solution)/shard_map/while/body/eval_jaxpr/hqk,qhd->khd/dot_general | solution.py:96
  708.0 60.0 %fusion.199 = bf16[2,512,4,64]{1,3,2,0:T(8,128)(2,1)} fusion(bf16[2,512,4,64]{1,3,2,0:T(8,128)(2,1)} %get-tuple-element.500, s32[]{:T(128)} %get-tuple-element.497, bf16[4096,4,64]{0,2,1:T(8,128)(2,1)S(1)} %get-tuple-element.517, f32[4,512,4096]{2,1,0:T(8,128)} %fusion.195, f32[4,512,4096]{2,1,0:T(8,128)} %fusion.196, ...), kind=kOutput, calls=%fused_computation.52.clone.1 | convolution fusion | flops 1166022656 | bytes 141050368 | tf_op jit(solution)/shard_map/while/body/eval_jaxpr/hqk,khd->qhd/dot_general | solution.py:93
  767.9 17.3 %fusion.198 = f32[4096,4,64]{0,2,1:T(8,128)} fusion(f32[4,512,4096]{2,1,0:T(8,128)} %fusion.196, f32[4,512]{1,0:T(4,128)S(1)} %dynamic-slice_bitcast_fusion.2, pred[512,4096]{1,0:T(8,128)(4,1)} %compare_and_fusion.3, f32[4096,4,64]{0,2,1:T(8,128)} %get-tuple-element.499, pred[]{:T(512)S(6)} %compare.3, ...), kind=kOutput, calls=%fused_computation.50.clone.1 | convolution fusion | flops 1109393408 | bytes 44310532 | tf_op jit(solution)/shard_map/while/body/eval_jaxpr/hqk,qhd->khd/dot_general | solution.py:99
  785.2 2.8 compare_and_fusion.3
  788.1 13.1 fusion.196
  801.2 13.1 fusion.195
  814.3 64.0 %fusion.197 = f32[4096,4,64]{0,2,1:T(8,128)} fusion(f32[4,512,4096]{2,1,0:T(8,128)} %fusion.195, f32[4,512,4096]{2,1,0:T(8,128)} %fusion.196, f32[4,512]{1,0:T(4,128)S(1)} %dynamic-slice_bitcast_fusion.2, pred[512,4096]{1,0:T(8,128)(4,1)} %compare_and_fusion.3, f32[4096,4,64]{0,2,1:T(8,128)} %get-tuple-element.498, pred[]{:T(512)S(6)} %compare.3, ...), kind=kOutput, calls=%fused_computation.48.clone.1 | convolution fusion | flops 1168119808 | bytes 147079680 | tf_op jit(solution)/shard_map/while/body/eval_jaxpr/hqk,qhd->khd/dot_general | solution.py:96
  878.3 60.0 %fusion.199 = bf16[2,512,4,64]{1,3,2,0:T(8,128)(2,1)} fusion(bf16[2,512,4,64]{1,3,2,0:T(8,128)(2,1)} %get-tuple-element.500, s32[]{:T(128)} %get-tuple-element.497, bf16[4096,4,64]{0,2,1:T(8,128)(2,1)S(1)} %get-tuple-element.517, f32[4,512,4096]{2,1,0:T(8,128)} %fusion.195, f32[4,512,4096]{2,1,0:T(8,128)} %fusion.196, ...), kind=kOutput, calls=%fused_computation.52.clone.1 | convolution fusion | flops 1166022656 | bytes 141050368 | tf_op jit(solution)/shard_map/while/body/eval_jaxpr/hqk,khd->qhd/dot_general | solution.py:93
  938.3 18.5 %fusion.198 = f32[4096,4,64]{0,2,1:T(8,128)} fusion(f32[4,512,4096]{2,1,0:T(8,128)} %fusion.196, f32[4,512]{1,0:T(4,128)S(1)} %dynamic-slice_bitcast_fusion.2, pred[512,4096]{1,0:T(8,128)(4,1)} %compare_and_fusion.3, f32[4096,4,64]{0,2,1:T(8,128)} %get-tuple-element.499, pred[]{:T(512)S(6)} %compare.3, ...), kind=kOutput, calls=%fused_computation.50.clone.1 | convolution fusion | flops 1109393408 | bytes 44310532 | tf_op jit(solution)/shard_map/while/body/eval_jaxpr/hqk,qhd->khd/dot_general | solution.py:99
  956.9 5.6 copy.61
  962.7 5.6 copy.60
  969.5 4.1 fusion.120
  973.7 6.6 fusion.118
  981.9 6.7 fusion.121
  992.0 47.7 %reduce-scatter.15.cloned.1.call-done = f32[1024,256]{1,0:T(8,128)} async-done(((f32[4096,256]{1,0:T(8,128)}), f32[1024,256]{1,0:T(8,128)}) %reduce-scatter.15.cloned.1.call-update) | async-done | bytes 1048592 | tf_op jit(solution)/shard_map/reduce_scatter | solution.py:184
  1040.9 78.2 %reduce-scatter.13.cloned.1.call-done = f32[1024,256]{1,0:T(8,128)} async-done(((f32[4096,256]{1,0:T(8,128)}), f32[1024,256]{1,0:T(8,128)}) %reduce-scatter.13.cloned.1.call-update) | async-done | bytes 1048592 | tf_op jit(solution)/shard_map/reduce_scatter | solution.py:181
  1121.2 4.5 fusion.105
  1128.1 5.3 convolution_bitcast_fusion
  1133.5 9.4 reduce-scatter.19.cloned.1.call-done
  1142.9 56.5 %reduce-scatter.23.cloned.1.call-done = f32[1024,512]{1,0:T(8,128)} async-done(((f32[1024,1024]{1,0:T(8,128)}), f32[1024,512]{1,0:T(8,128)}) %reduce-scatter.23.cloned.1.call-update) | async-done | bytes 2097168 | tf_op jit(solution)/shard_map/reduce_scatter | solution.py:204
  1199.4 56.7 %reduce-scatter.21.cloned.1.call-done = f32[512,1024]{1,0:T(8,128)} async-done(((f32[1024,1024]{1,0:T(8,128)}), f32[512,1024]{1,0:T(8,128)}) %reduce-scatter.21.cloned.1.call-update) | async-done | bytes 2097168 | tf_op jit(solution)/shard_map/reduce_scatter | solution.py:203
  1256.1 45.5 %reduce-scatter.17.cloned.1.call-done = f32[3,512,256]{1,2,0:T(8,128)} async-done(((f32[3,1024,256]{1,2,0:T(8,128)}), f32[3,512,256]{1,2,0:T(8,128)}) %reduce-scatter.17.cloned.1.call-update) | async-done | bytes 1572880 | tf_op jit(solution)/shard_map/reduce_scatter | solution.py:201
  1301.6 17.3 %reduce-scatter.25.cloned.1.call-done = f32[512,2]{1,0:T(8,128)} async-done(((f32[1024,2]{1,0:T(8,128)}), f32[512,2]{1,0:T(8,128)}) %reduce-scatter.25.cloned.1.call-update) | async-done | bytes 4112
  1320.0 16.2 reduce-scatter.27.cloned.1.call-done
  1337.2 12.4 all-reduce
  1349.7 74.4 %all-reduce.14.cloned.1.call-done = f32[1024,1024]{1,0:T(8,128)} async-done(((f32[1024,1024]{1,0:T(8,128)}), f32[1024,1024]{1,0:T(8,128)}) %all-reduce.14.cloned.1.call-update) | async-done | bytes 4194320 | tf_op jit(solution)/shard_map/psum | solution.py:36
  1424.0 5.2 add_convert_fusion
  1429.2 221.3 %all-reduce.16.cloned.1.call-done = (f32[3,512,256]{1,2,0:T(8,128)}, f32[256,512]{1,0:T(8,128)}, f32[512,1024]{1,0:T(8,128)}, f32[1024,512]{1,0:T(8,128)}) async-done(((f32[3,512,256]{1,2,0:T(8,128)}, f32[256,512]{1,0:T(8,128)}, f32[512,1024]{1,0:T(8,128)}, f32[1024,512]{1,0:T(8,128)}), (f32[3,512,256]{1,2,0:T(8,128)}, f32[256,512]{1,0:T(8,128)}, f32[512,1024]{1,0:T(8,128)}, ...) | async-done | bytes 6291472 | tf_op jit(solution)/shard_map/psum | solution.py:208
  1650.5 3.2 copy.65
  1655.6 3.2 copy.110
  (186 shorter events, 46.0 us)
Async XLA Ops:
  7.2 32.9 %all-gather.8.cloned.1.call-start = ((), (), s32[]{:S(2)}) async-start(), calls=%async_computation.8 | async-start | bytes 2359296 | tf_op jit(solution)/shard_map/all_gather | solution.py:111
  9.5 81.6 %all-gather.14.cloned.1.call-start = ((), (), s32[]{:S(2)}) async-start(), calls=%async_computation.21 | async-start | bytes 2621440 | tf_op jit(solution)/shard_map/all_gather | solution.py:133
  44.0 1.9 copy-start.37
  44.0 2.3 copy-start.16
  45.1 92.9 %all-gather.16.cloned.1.call-start = ((), (), s32[]{:S(2)}) async-start(), calls=%async_computation.22 | async-start | bytes 2621440 | tf_op jit(solution)/shard_map/all_gather | solution.py:134
  45.8 281.7 %all-reduce.8.cloned.1.call-start = ((), (), s32[]{:S(2)}) async-start(), calls=%async_computation.9 | async-start | bytes 8388608 | tf_op jit(solution)/shard_map/psum | solution.py:36
  138.0 102.4 %copy-start.11 = (bf16[256,1024]{1,0:T(8,128)(2,1)S(1)}, bf16[256,1024]{1,0:T(8,128)(2,1)}, u32[]{:S(2)}) copy-start(bf16[256,1024]{1,0:T(8,128)(2,1)} %all_gather.31) | copy-start | bytes 1572868
  239.6 0.8 copy-start.7
  243.1 1.2 copy-start.33
  243.1 5.6 copy-start.34
  243.1 84.4 %copy-start.9 = (bf16[1024,1024]{1,0:T(8,128)(2,1)S(1)}, bf16[1024,1024]{1,0:T(8,128)(2,1)}, u32[]{:S(2)}) copy-start(bf16[1024,1024]{1,0:T(8,128)(2,1)} %param.13) | copy-start | bytes 6291460
  243.2 119.1 %all-gather.10.cloned.1.call-start = ((), (), s32[]{:S(2)}) async-start(), calls=%async_computation.10 | async-start | bytes 3145728 | tf_op jit(solution)/shard_map/all_gather | solution.py:113
  243.7 153.1 %all-gather.12.cloned.1.call-start = ((), (), s32[]{:S(2)}) async-start(), calls=%async_computation.11 | async-start | bytes 3145728 | tf_op jit(solution)/shard_map/all_gather | solution.py:114
  244.3 244.7 %all-reduce.10.cloned.1.call-start = ((), (), s32[]{:S(2)}) async-start(), calls=%async_computation.12 | async-start | bytes 8388608 | tf_op jit(solution)/shard_map/psum | solution.py:36
  248.7 356.8 %copy-start.21 = (f32[1,1024]{1,0:T(1,128)}, f32[1,1024]{1,0:T(1,128)S(1)}, u32[]{:S(2)}) copy-start(f32[1,1024]{1,0:T(1,128)S(1)} %get-tuple-element.329) | copy-start | bytes 12292
  253.3 235.7 %copy-start.28 = (f32[1,1024]{1,0:T(1,128)}, f32[1,1024]{1,0:T(1,128)S(1)}, u32[]{:S(2)}) copy-start(f32[1,1024]{1,0:T(1,128)S(1)} %get-tuple-element.331) | copy-start | bytes 12292
  330.2 2.0 copy-start
  330.2 275.3 %copy-start.17 = (f32[1024]{0:T(1024)}, f32[1024]{0:T(1024)S(1)}, u32[]{:S(2)}) copy-start(f32[1024]{0:T(1024)S(1)} %broadcast_multiply_fusion.1) | copy-start | bytes 12292
  332.7 272.8 %copy-start.19 = (f32[1024]{0:T(1024)}, f32[1024]{0:T(1024)S(1)}, u32[]{:S(2)}) copy-start(f32[1024]{0:T(1024)S(1)} %fusion.114) | copy-start | bytes 12292
  403.4 195.7 %all-reduce.12.cloned.1.call-start = ((), (), s32[]{:S(2)}) async-start(), calls=%async_computation.13 | async-start | bytes 8388608 | tf_op jit(solution)/shard_map/psum | solution.py:36
  493.3 1.6 copy-start.6
  497.4 3.2 copy-start.36
  497.4 3.2 copy-start.38
  497.4 6.3 copy-start.39
  500.6 7.0 copy-start.5
  500.6 98.5 %copy-start.25 = (f32[1024]{0:T(1024)}, f32[1024]{0:T(1024)S(1)}, u32[]{:S(2)}) copy-start(f32[1024]{0:T(1024)S(1)} %negate_multiply_fusion.2) | copy-start | bytes 12292
  503.7 5.2 copy-start.35
  507.6 1.3 copy-start.41
  513.3 526.3 %reduce-scatter.15.cloned.1.call-start = ((), (), s32[]{:S(2)}) async-start(), calls=%async_computation.15 | async-start | bytes 5242880 | tf_op jit(solution)/shard_map/reduce_scatter | solution.py:184
  599.1 6.4 copy-start.1
  607.2 2.0 copy-start.4
  607.3 7.9 copy-start.23
  609.2 5.9 copy-start.2
  618.2 13.1 copy-start.3
  788.1 13.1 copy-start.3
  962.6 156.5 %reduce-scatter.13.cloned.1.call-start = ((), (), s32[]{:S(2)}) async-start(), calls=%async_computation.14 | async-start | bytes 5242880 | tf_op jit(solution)/shard_map/reduce_scatter | solution.py:181
  968.3 1.2 copy-start.8
  968.3 1.2 copy-start.24
  968.3 5.4 copy-start.26
  968.3 5.4 copy-start.40
  968.3 174.5 %reduce-scatter.19.cloned.1.call-start = ((), (), s32[]{:S(2)}) async-start(), calls=%async_computation.18 | async-start | bytes 1572864 | tf_op jit(solution)/shard_map/reduce_scatter | solution.py:202
  973.6 225.7 %reduce-scatter.23.cloned.1.call-start = ((), (), s32[]{:S(2)}) async-start(), calls=%async_computation.20 | async-start | bytes 6291456 | tf_op jit(solution)/shard_map/reduce_scatter | solution.py:204
  980.3 0.7 copy-start.18
  980.3 0.7 copy-start.20
  980.3 0.7 copy-start.22
  980.3 0.7 copy-start.29
  980.3 1.6 copy-start.42
  980.4 275.7 %reduce-scatter.21.cloned.1.call-start = ((), (), s32[]{:S(2)}) async-start(), calls=%async_computation.19 | async-start | bytes 6291456 | tf_op jit(solution)/shard_map/reduce_scatter | solution.py:203
  988.7 132.5 %copy-start.10 = (bf16[1024,1024]{1,0:T(8,128)(2,1)S(1)}, bf16[1024,1024]{1,0:T(8,128)(2,1)}, u32[]{:S(2)}) copy-start(bf16[1024,1024]{1,0:T(8,128)(2,1)} %param.13) | copy-start | bytes 6291460
  988.7 312.8 %reduce-scatter.17.cloned.1.call-start = ((), (), s32[]{:S(2)}) async-start(), calls=%async_computation.17 | async-start | bytes 4718592 | tf_op jit(solution)/shard_map/reduce_scatter | solution.py:201
  1120.4 0.8 copy-start.14
  1121.2 4.6 copy-start.30
  1121.2 4.6 copy-start.32
  1125.7 1.2 copy-start.27
  1125.7 1.2 copy-start.31
  1125.7 2.4 copy-start.13
  1125.7 2.4 copy-start.15
  1125.8 193.1 %reduce-scatter.25.cloned.1.call-start = ((), (), s32[]{:S(2)}) async-start(), calls=%async_computation.23 | async-start | bytes 786432
  1126.9 209.2 %reduce-scatter.27.cloned.1.call-start = ((), (), s32[]{:S(2)}) async-start(), calls=%async_computation.24 | async-start | bytes 786432
  1128.0 296.0 %all-reduce.14.cloned.1.call-start = ((), (), s32[]{:S(2)}) async-start(), calls=%async_computation.16 | async-start | bytes 8388608 | tf_op jit(solution)/shard_map/psum | solution.py:36
  1133.4 517.1 %all-reduce.16.cloned.1.call-start = ((), (), s32[]{:S(2)}) async-start(), calls=%async_computation.25 | async-start | bytes 12582912 | tf_op jit(solution)/shard_map/psum | solution.py:208
  1650.5 8.2 copy-start.12
Sparse Core Ops, SparseCore 0:
  10.1 29.8 all-gather.7
  45.2 45.9 all-gather.13
  93.3 44.6 all-gather.15
  243.3 84.1 all-reduce.7
  329.0 33.2 all-gather.9
  363.7 33.1 all-gather.11
  403.5 85.4 all-reduce.9
  513.5 85.6 all-reduce.11
  962.7 76.8 reduce-scatter.14
  1041.8 77.2 reduce-scatter.12
  1122.0 20.8 reduce-scatter.18
  1145.0 54.3 reduce-scatter.22
  1201.8 54.2 reduce-scatter.20
  1258.2 43.3 reduce-scatter.16
  1304.3 14.5 reduce-scatter.24
  1321.6 14.5 reduce-scatter.26
  1338.5 85.4 all-reduce.13
  1426.5 223.9 all-reduce.15
where the time goes:
time: 1670 us
  waiting for transfers between devices  1030 us (62%)
  matrix products  465 us (28%)
  other arithmetic  71.4 us (4%)
  local copies, waits for them, and re-layouts  51.7 us (3%)
  blocking collectives  30.3 us (2%)
    psum x4, waiting for transfers between devices, tp_total(): return lax.psum(terms, 'tp')  319 us
    psum x1, waiting for transfers between devices, body(): lax.psum((qkv_grad, out_proj_grad, up_grad, down_grad, gain_grad, shift_g...  221 us
    dot_general x2, matrix products, one_block(): jnp.einsum('hqk,qhd->khd', grad_scores, query_block, preferred_element_ty...  128 us
    dot_general x2, matrix products, one_block(): jnp.einsum('hqk,khd->qhd', grad_scores, key_heads, preferred_element_type...  120 us
    reduce_scatter x1, waiting for transfers between devices, body(): lax.psum_scatter(key_grad.reshape(pack_rows, local_width), 'ctx', scatter...  78.2 us
    dot_general x4, matrix products, score_block(): jnp.einsum('qhd,khd->hqk', query_block, key_heads, preferred_element_type...  57.8 us
    reduce_scatter x1, waiting for transfers between devices, body(): lax.psum_scatter(up_grad, 'fsdp', scatter_dimension=0, tiled=True)  56.7 us
    reduce_scatter x1, waiting for transfers between devices, body(): lax.psum_scatter(down_grad, 'fsdp', scatter_dimension=1, tiled=True)  56.5 us
  transfers between devices with their start and end apart: 18, of which 18 were waited for; matrix products, arithmetic and copies ran while one was open for 4% of the time, Pallas kernels for 0%

commit v1 on v0

--- a/solution.py
+++ b/solution.py
@@ -1,3 +1,4 @@
+import functools
 import math
 import jax
 import jax.numpy as jnp
@@ -8,6 +9,34 @@
 SEQS = 3
 norm_eps = 1e-12
 masked_low = -1e30
+
+
+def attach_hubs(frame_in, across):
+    x_next = lax.axis_size(across)
+    p_next = lax.axis_index(across)
+    left_arr, h_now, mixed_arr = (x_next, p_next, frame_in.shape[0])
+    cards = [(tick, (tick + 1) % left_arr) for tick in range(left_arr)]
+    rack = [(tick, (tick - 1) % left_arr) for tick in range(left_arr)]
+    w_next = jnp.zeros(
+        (*frame_in.shape[:0], left_arr * mixed_arr, *frame_in.shape[1:]), frame_in.dtype
+    )
+    w_next = lax.dynamic_update_slice_in_dim(w_next, frame_in, h_now * mixed_arr, axis=0)
+    main = res = frame_in
+    taken_in = left_arr // 2
+    for ix in range(1, taken_in + 1):
+        main = lax.ppermute(main, across, cards)
+        w_next = lax.dynamic_update_slice_in_dim(
+            w_next, main, (h_now - ix) % left_arr * mixed_arr, axis=0
+        )
+        if ix < left_arr - taken_in:
+            res = lax.ppermute(res, across, rack)
+            w_next = lax.dynamic_update_slice_in_dim(
+                w_next, res, (h_now + ix) % left_arr * mixed_arr, axis=0
+            )
+    return w_next
+
+
+search_ends_now = functools.partial(attach_hubs, across="ctx")
 
 
 def layer_norm(rows, gain, shift):
@@ -130,7 +159,7 @@
         "td,sdc->stc", tokens, full_qkv, preferred_element_type=jnp.float32
     ).astype(jnp.bfloat16)
     key_rows, value_rows = (
-        lax.all_gather(projected[1], "ctx", axis=0, tiled=True),
+        search_ends_now(projected[1]),
         lax.all_gather(projected[2], "ctx", axis=0, tiled=True),
     )
     key_heads = key_rows.reshape(pack_rows, local_heads, HEAD_DIM)

time: 1670 us -> 1650 us (0.988)
  waiting for transfers between devices: 1030 us -> 991 us
    all_gather x1, waiting for transfers between devices: 46.9 us -> 5.14 us  [body(): lax.all_gather(projected[2], 'ctx', axis=0, tiled=True)]
    ppermute x0 -> x3, waiting for transfers between devices: none -> 36 us  [the longest x1 18.4 us: attach_hubs(): res = lax.ppermute(res, across, rack)]
    all_gather x1 -> x0, waiting for transfers between devices: 35.5 us -> none  [body(): lax.all_gather(projected[1], 'ctx', axis=0, tiled=True)]
    unnamed x20 -> x19, waiting for transfers between devices: 35.5 us -> 34.8 us
  transfers between devices with their start and end apart: 18 -> 20, of which waited for: 18 -> 20; matrix products, arithmetic and copies ran while one was open for 4% -> 5% of each run, Pallas kernels for 0% -> 0%
where the time goes in v1:
time: 1650 us
  waiting for transfers between devices  991 us (60%)
  matrix products  468 us (28%)
  other arithmetic  71.4 us (4%)
  local copies, waits for them, and re-layouts  58.6 us (4%)
  blocking collectives  29.5 us (2%)
    psum x4, waiting for transfers between devices, tp_total(): return lax.psum(terms, 'tp')  321 us
    psum x1, waiting for transfers between devices, body(): lax.psum((qkv_grad, out_proj_grad, up_grad, down_grad, gain_grad, shift_g...  221 us
    dot_general x2, matrix products, one_block(): jnp.einsum('hqk,qhd->khd', grad_scores, query_block, preferred_element_ty...  127 us
    dot_general x2, matrix products, one_block(): jnp.einsum('hqk,khd->qhd', grad_scores, key_heads, preferred_element_type...  121 us
    reduce_scatter x1, waiting for transfers between devices, body(): lax.psum_scatter(key_grad.reshape(pack_rows, local_width), 'ctx', scatter...  78.3 us
    dot_general x4, matrix products, score_block(): jnp.einsum('qhd,khd->hqk', query_block, key_heads, preferred_element_type...  60.9 us
    reduce_scatter x1, waiting for transfers between devices, body(): lax.psum_scatter(down_grad, 'fsdp', scatter_dimension=1, tiled=True)  56.7 us
    reduce_scatter x1, waiting for transfers between devices, body(): lax.psum_scatter(up_grad, 'fsdp', scatter_dimension=0, tiled=True)  56.6 us
  transfers between devices with their start and end apart: 20, of which 20 were waited for; matrix products, arithmetic and copies ran while one was open for 5% of the time, Pallas kernels for 0%

profile of v1, /device:TPU:0, one launch (start us, length us, event | category | flops | bytes accessed | tf_op | source)
XLA Modules:
  0.0 1650.5 jit_solution(7366118310210114163)
XLA Ops:
  9.6 30.5 %all-gather.6.cloned.1.call-done = bf16[3,1024,256]{1,2,0:T(8,128)(2,1)} async-done(((bf16[3,512,256]{1,2,0:T(8,128)(2,1)}), bf16[3,1024,256]{1,2,0:T(8,128)(2,1)}) %all-gather.6.cloned.1.call-update) | async-done | bytes 1572880 | tf_op jit(solution)/shard_map/all_gather | solution.py:140
  40.1 3.9 fusion.111
  49.0 8.3 all_gather.27
  57.4 9.0 collective-permute-done
  66.5 11.2 collective-permute-start.2
  81.5 18.4 %collective-permute-done.1 = bf16[1024,256]{0,1:T(8,128)(2,1)} collective-permute-done((bf16[1024,256]{0,1:T(8,128)(2,1)}, bf16[1024,256]{0,1:T(8,128)(2,1)}, u32[]{:S(2)}, u32[]{:S(2)}) %collective-permute-start.1) | collective-permute-done | bytes 524320 | tf_op jit(solution)/shard_map/ppermute | solution.py:32
  101.8 8.6 collective-permute-done.2
  112.3 5.1 all-gather.12.cloned.1.call-done
  117.4 99.8 %while.27 = (s32[]{:T(128)}, bf16[2,512,4,64]{1,3,2,0:T(8,128)(2,1)}, f32[2,4,512]{2,1,0:T(4,128)S(1)}, s32[2,512]{1,0:T(2,128)S(1)}, s32[4096]{0:T(1024)S(1)}, ...) while((s32[]{:T(128)}, ...), condition=%wide.region_6.7_spmd, body=%wide.region_2.6_spmd.sunk | while | flops 2271357440 | bytes 113924704 | solution.py:102
  119.7 15.8 fusion.181
  135.5 15.6 fusion.182
  151.1 16.2 fusion.183
  169.6 15.8 fusion.181
  185.4 15.6 fusion.182
  201.0 16.2 fusion.183
  223.7 4.3 all_gather.28
  228.1 4.6 all_gather.29
  232.6 75.3 %all-reduce.8.cloned.1.call-done = f32[1024,1024]{1,0:T(8,128)} async-done(((f32[1024,1024]{1,0:T(8,128)}), f32[1024,1024]{1,0:T(8,128)}) %all-reduce.8.cloned.1.call-update) | async-done | bytes 4194320 | tf_op jit(solution)/shard_map/psum | solution.py:65
  313.1 29.5 %all-gather.8.cloned.1.call-done = bf16[1024,1024]{1,0:T(8,128)(2,1)} async-done(((bf16[512,1024]{1,0:T(8,128)(2,1)}), bf16[1024,1024]{1,0:T(8,128)(2,1)}) %all-gather.8.cloned.1.call-update) | async-done | bytes 2097168 | tf_op jit(solution)/shard_map/all_gather | solution.py:142
  342.7 15.5 multiply_convert_fusion.1
  358.2 19.1 %all-gather.10.cloned.1.call-done = bf16[1024,1024]{1,0:T(8,128)(2,1)} async-done(((bf16[1024,512]{1,0:T(8,128)(2,1)}), bf16[1024,1024]{1,0:T(8,128)(2,1)}) %all-gather.10.cloned.1.call-update) | async-done | bytes 2097168 | tf_op jit(solution)/shard_map/all_gather | solution.py:143
  377.3 6.5 fusion.135
  384.3 85.2 %all-reduce.10.cloned.1.call-done = f32[1024,1024]{1,0:T(8,128)} async-done(((f32[1024,1024]{1,0:T(8,128)}), f32[1024,1024]{1,0:T(8,128)}) %all-reduce.10.cloned.1.call-update) | async-done | bytes 4194320 | tf_op jit(solution)/shard_map/psum | solution.py:65
  469.5 4.2 fusion.127
  477.9 3.2 fusion.126
  481.1 3.1 copy-done.38
  484.2 3.9 add_convert_fusion.1
  489.4 4.3 fusion.136
  493.8 85.7 %all-reduce.12.cloned.1.call-done = f32[1024,1024]{1,0:T(8,128)} async-done(((f32[1024,1024]{1,0:T(8,128)}), f32[1024,1024]{1,0:T(8,128)}) %all-reduce.12.cloned.1.call-update) | async-done | bytes 4194320 | tf_op jit(solution)/shard_map/psum | solution.py:65
  579.5 6.4 multiply_reduce_fusion.1
  595.6 344.9 %while.28 = (s32[]{:T(128)}, f32[4096,4,64]{0,2,1:T(8,128)}, f32[4096,4,64]{0,2,1:T(8,128)}, bf16[2,512,4,64]{1,3,2,0:T(8,128)(2,1)}, bf16[2,512,4,64]{1,3,2,0:T...) while((s32[]{:T(128)}, f32[4096,4,64]{0,2,1:T(8,128)}, ...), condition=%wide.region_20.21_spmd.clone, body=%wide.region_18.20_spmd.clone.sunk | while | flops 5595217920 | bytes 406428800 | solution.py:133
  595.8 2.8 compare_and_fusion.3
  598.7 14.7 fusion.196
  613.3 13.1 fusion.195
  626.4 63.2 %fusion.197 = f32[4096,4,64]{0,2,1:T(8,128)} fusion(f32[4,512,4096]{2,1,0:T(8,128)} %fusion.195, f32[4,512,4096]{2,1,0:T(8,128)} %fusion.196, f32[4,512]{1,0:T(4,128)S(1)} %dynamic-slice_bitcast_fusion.2, pred[512,4096]{1,0:T(8,128)(4,1)} %compare_and_fusion.3, f32[4096,4,64]{0,2,1:T(8,128)} %get-tuple-element.498, pred[]{:T(512)S(6)} %compare.6, ...), kind=kOutput, calls=%fused_computation.48.clone.1 | convolution fusion | flops 1168119808 | bytes 147079680 | tf_op jit(solution)/shard_map/while/body/eval_jaxpr/hqk,qhd->khd/dot_general | solution.py:125
  689.6 60.3 %fusion.199 = bf16[2,512,4,64]{1,3,2,0:T(8,128)(2,1)} fusion(bf16[2,512,4,64]{1,3,2,0:T(8,128)(2,1)} %get-tuple-element.500, s32[]{:T(128)} %get-tuple-element.497, bf16[4096,4,64]{0,2,1:T(8,128)(2,1)} %get-tuple-element.517, f32[4,512,4096]{2,1,0:T(8,128)} %fusion.195, f32[4,512,4096]{2,1,0:T(8,128)} %fusion.196, ...), kind=kOutput, calls=%fused_computation.52.clone.1 | convolution fusion | flops 1166022656 | bytes 141050368 | tf_op jit(solution)/shard_map/while/body/eval_jaxpr/hqk,khd->qhd/dot_general | solution.py:122
  749.9 17.4 %fusion.198 = f32[4096,4,64]{0,2,1:T(8,128)} fusion(f32[4,512,4096]{2,1,0:T(8,128)} %fusion.196, f32[4,512]{1,0:T(4,128)S(1)} %dynamic-slice_bitcast_fusion.2, pred[512,4096]{1,0:T(8,128)(4,1)} %compare_and_fusion.3, f32[4096,4,64]{0,2,1:T(8,128)} %get-tuple-element.499, pred[]{:T(512)S(6)} %compare.6, ...), kind=kOutput, calls=%fused_computation.50.clone.1 | convolution fusion | flops 1109393408 | bytes 44310532 | tf_op jit(solution)/shard_map/while/body/eval_jaxpr/hqk,qhd->khd/dot_general | solution.py:128
  767.3 2.8 compare_and_fusion.3
  770.1 14.7 fusion.196
  784.8 13.1 fusion.195
  797.9 63.6 %fusion.197 = f32[4096,4,64]{0,2,1:T(8,128)} fusion(f32[4,512,4096]{2,1,0:T(8,128)} %fusion.195, f32[4,512,4096]{2,1,0:T(8,128)} %fusion.196, f32[4,512]{1,0:T(4,128)S(1)} %dynamic-slice_bitcast_fusion.2, pred[512,4096]{1,0:T(8,128)(4,1)} %compare_and_fusion.3, f32[4096,4,64]{0,2,1:T(8,128)} %get-tuple-element.498, pred[]{:T(512)S(6)} %compare.6, ...), kind=kOutput, calls=%fused_computation.48.clone.1 | convolution fusion | flops 1168119808 | bytes 147079680 | tf_op jit(solution)/shard_map/while/body/eval_jaxpr/hqk,qhd->khd/dot_general | solution.py:125
  861.5 60.3 %fusion.199 = bf16[2,512,4,64]{1,3,2,0:T(8,128)(2,1)} fusion(bf16[2,512,4,64]{1,3,2,0:T(8,128)(2,1)} %get-tuple-element.500, s32[]{:T(128)} %get-tuple-element.497, bf16[4096,4,64]{0,2,1:T(8,128)(2,1)} %get-tuple-element.517, f32[4,512,4096]{2,1,0:T(8,128)} %fusion.195, f32[4,512,4096]{2,1,0:T(8,128)} %fusion.196, ...), kind=kOutput, calls=%fused_computation.52.clone.1 | convolution fusion | flops 1166022656 | bytes 141050368 | tf_op jit(solution)/shard_map/while/body/eval_jaxpr/hqk,khd->qhd/dot_general | solution.py:122
  921.8 18.5 %fusion.198 = f32[4096,4,64]{0,2,1:T(8,128)} fusion(f32[4,512,4096]{2,1,0:T(8,128)} %fusion.196, f32[4,512]{1,0:T(4,128)S(1)} %dynamic-slice_bitcast_fusion.2, pred[512,4096]{1,0:T(8,128)(4,1)} %compare_and_fusion.3, f32[4096,4,64]{0,2,1:T(8,128)} %get-tuple-element.499, pred[]{:T(512)S(6)} %compare.6, ...), kind=kOutput, calls=%fused_computation.50.clone.1 | convolution fusion | flops 1109393408 | bytes 44310532 | tf_op jit(solution)/shard_map/while/body/eval_jaxpr/hqk,qhd->khd/dot_general | solution.py:128
  940.5 5.7 copy.61
  946.2 5.6 copy.60
  953.0 4.1 fusion.120
  957.3 6.6 fusion.118
  965.5 6.8 fusion.121
  975.6 47.7 %reduce-scatter.15.cloned.1.call-done = f32[1024,256]{1,0:T(8,128)} async-done(((f32[4096,256]{1,0:T(8,128)}), f32[1024,256]{1,0:T(8,128)}) %reduce-scatter.15.cloned.1.call-update) | async-done | bytes 1048592 | tf_op jit(solution)/shard_map/reduce_scatter | solution.py:213
  1024.5 78.3 %reduce-scatter.13.cloned.1.call-done = f32[1024,256]{1,0:T(8,128)} async-done(((f32[4096,256]{1,0:T(8,128)}), f32[1024,256]{1,0:T(8,128)}) %reduce-scatter.13.cloned.1.call-update) | async-done | bytes 1048592 | tf_op jit(solution)/shard_map/reduce_scatter | solution.py:210
  1104.9 4.5 fusion.105
  1111.8 5.2 convolution_bitcast_fusion
  1117.1 9.3 reduce-scatter.19.cloned.1.call-done
  1126.4 56.7 %reduce-scatter.23.cloned.1.call-done = f32[1024,512]{1,0:T(8,128)} async-done(((f32[1024,1024]{1,0:T(8,128)}), f32[1024,512]{1,0:T(8,128)}) %reduce-scatter.23.cloned.1.call-update) | async-done | bytes 2097168 | tf_op jit(solution)/shard_map/reduce_scatter | solution.py:233
  1183.1 56.6 %reduce-scatter.21.cloned.1.call-done = f32[512,1024]{1,0:T(8,128)} async-done(((f32[1024,1024]{1,0:T(8,128)}), f32[512,1024]{1,0:T(8,128)}) %reduce-scatter.21.cloned.1.call-update) | async-done | bytes 2097168 | tf_op jit(solution)/shard_map/reduce_scatter | solution.py:232
  1239.6 45.6 %reduce-scatter.17.cloned.1.call-done = f32[3,512,256]{1,2,0:T(8,128)} async-done(((f32[3,1024,256]{1,2,0:T(8,128)}), f32[3,512,256]{1,2,0:T(8,128)}) %reduce-scatter.17.cloned.1.call-update) | async-done | bytes 1572880 | tf_op jit(solution)/shard_map/reduce_scatter | solution.py:230
  1285.3 17.3 %reduce-scatter.27.cloned.1.call-done = f32[512,2]{1,0:T(8,128)} async-done(((f32[1024,2]{1,0:T(8,128)}), f32[512,2]{1,0:T(8,128)}) %reduce-scatter.27.cloned.1.call-update) | async-done | bytes 4112
  1303.7 16.2 reduce-scatter.25.cloned.1.call-done
  1321.0 12.4 all-reduce
  1333.3 74.4 %all-reduce.14.cloned.1.call-done = f32[1024,1024]{1,0:T(8,128)} async-done(((f32[1024,1024]{1,0:T(8,128)}), f32[1024,1024]{1,0:T(8,128)}) %all-reduce.14.cloned.1.call-update) | async-done | bytes 4194320 | tf_op jit(solution)/shard_map/psum | solution.py:65
  1407.8 5.2 add_convert_fusion
  1413.0 221.3 %all-reduce.16.cloned.1.call-done = (f32[3,512,256]{1,2,0:T(8,128)}, f32[256,512]{1,0:T(8,128)}, f32[512,1024]{1,0:T(8,128)}, f32[1024,512]{1,0:T(8,128)}) async-done(((f32[3,512,256]{1,2,0:T(8,128)}, f32[256,512]{1,0:T(8,128)}, f32[512,1024]{1,0:T(8,128)}, f32[1024,512]{1,0:T(8,128)}), (f32[3,512,256]{1,2,0:T(8,128)}, f32[256,512]{1,0:T(8,128)}, f32[512,1024]{1,0:T(8,128)}, ...) | async-done | bytes 6291472 | tf_op jit(solution)/shard_map/psum | solution.py:237
  1634.3 3.2 copy.65
  1639.3 3.2 copy.114
  (190 shorter events, 64.2 us)
Async XLA Ops:
  7.2 32.9 %all-gather.6.cloned.1.call-start = ((), (), s32[]{:S(2)}) async-start(), calls=%async_computation.8 | async-start | bytes 2359296 | tf_op jit(solution)/shard_map/all_gather | solution.py:140
  9.5 39.5 %copy-start.15 = (bf16[256,512]{1,0:T(8,128)(2,1)S(1)}, bf16[256,512]{1,0:T(8,128)(2,1)}, u32[]{:S(2)}) copy-start(bf16[256,512]{1,0:T(8,128)(2,1)} %param.15) | copy-start | bytes 786436
  9.5 107.9 %all-gather.12.cloned.1.call-start = ((), (), s32[]{:S(2)}) async-start(), calls=%async_computation.21 | async-start | bytes 2621440 | tf_op jit(solution)/shard_map/all_gather | solution.py:163
  44.0 13.3 copy-start.36
  45.1 262.8 %all-reduce.8.cloned.1.call-start = ((), (), s32[]{:S(2)}) async-start(), calls=%async_computation.9 | async-start | bytes 8388608 | tf_op jit(solution)/shard_map/psum | solution.py:65
  45.1 21.3 %collective-permute-start = (bf16[1024,256]{0,1:T(8,128)(2,1)}, bf16[1024,256]{0,1:T(8,128)(2,1)S(1)}, u32[]{:S(2)}, u32[]{:S(2)}) collective-permute-start(bf16[1024,256]{0,1:T(8,128)(2,1)} %get-tuple-element.326), channel_id=1, source_target_pairs={{0,4},{4,8},{8,12},{12,0},{1,5},{5,9},{9,13},{13,1},{2,6},{6,10},{... | collective-permute-start | bytes 1572872 | tf_op jit(solution)/shard_map/ppermute | solution.py:27
  46.7 53.3 %collective-permute-start.1 = (bf16[1024,256]{0,1:T(8,128)(2,1)}, bf16[1024,256]{0,1:T(8,128)(2,1)}, u32[]{:S(2)}, u32[]{:S(2)}) collective-permute-start(bf16[1024,256]{0,1:T(8,128)(2,1)} %get-tuple-element.326), channel_id=1, source_target_pairs={{0,12},{4,0},{8,4},{12,8},{1,13},{5,1},{9,5},{13,9},{2,14},{6,2},{... | collective-permute-start | bytes 1572872 | tf_op jit(solution)/shard_map/ppermute | solution.py:32
  66.5 43.9 %collective-permute-start.2 = (bf16[1024,256]{0,1:T(8,128)(2,1)S(1)}, bf16[1024,256]{0,1:T(8,128)(2,1)}, u32[]{:S(2)}, u32[]{:S(2)}) collective-permute-start(bf16[1024,256]{0,1:T(8,128)(2,1)S(1)} %collective-permute-done), channel_id=1, source_target_pairs={{0,4},{4,8},{8,12},{12,0},{1,5},{5,9},{9,13},{13,1},{2,6},{6,10},{... | collective-permute-start | bytes 1572872 | tf_op jit(solution)/shard_map/ppermute | solution.py:27
  117.4 102.3 %copy-start.10 = (bf16[256,1024]{1,0:T(8,128)(2,1)S(1)}, bf16[256,1024]{1,0:T(8,128)(2,1)}, u32[]{:S(2)}) copy-start(bf16[256,1024]{1,0:T(8,128)(2,1)} %all_gather.27) | copy-start | bytes 1572868
  218.9 0.8 copy-start.6
  222.4 1.2 copy-start.32
  222.4 5.6 copy-start.33
  222.4 85.5 %copy-start.8 = (bf16[1024,1024]{1,0:T(8,128)(2,1)S(1)}, bf16[1024,1024]{1,0:T(8,128)(2,1)}, u32[]{:S(2)}) copy-start(bf16[1024,1024]{1,0:T(8,128)(2,1)} %param.13) | copy-start | bytes 6291460
  222.5 120.2 %all-gather.8.cloned.1.call-start = ((), (), s32[]{:S(2)}) async-start(), calls=%async_computation.10 | async-start | bytes 3145728 | tf_op jit(solution)/shard_map/all_gather | solution.py:142
  223.1 154.2 %all-gather.10.cloned.1.call-start = ((), (), s32[]{:S(2)}) async-start(), calls=%async_computation.11 | async-start | bytes 3145728 | tf_op jit(solution)/shard_map/all_gather | solution.py:143
  223.6 245.8 %all-reduce.10.cloned.1.call-start = ((), (), s32[]{:S(2)}) async-start(), calls=%async_computation.12 | async-start | bytes 8388608 | tf_op jit(solution)/shard_map/psum | solution.py:65
  228.1 357.9 %copy-start.20 = (f32[1,1024]{1,0:T(1,128)}, f32[1,1024]{1,0:T(1,128)S(1)}, u32[]{:S(2)}) copy-start(f32[1,1024]{1,0:T(1,128)S(1)} %get-tuple-element.329) | copy-start | bytes 12292
  232.6 236.8 %copy-start.27 = (f32[1,1024]{1,0:T(1,128)}, f32[1,1024]{1,0:T(1,128)S(1)}, u32[]{:S(2)}) copy-start(f32[1,1024]{1,0:T(1,128)S(1)} %get-tuple-element.331) | copy-start | bytes 12292
  310.6 2.0 copy-start
  310.6 275.3 %copy-start.16 = (f32[1024]{0:T(1024)}, f32[1024]{0:T(1024)S(1)}, u32[]{:S(2)}) copy-start(f32[1024]{0:T(1024)S(1)} %broadcast_multiply_fusion.1) | copy-start | bytes 12292
  313.1 272.8 %copy-start.18 = (f32[1024]{0:T(1024)}, f32[1024]{0:T(1024)S(1)}, u32[]{:S(2)}) copy-start(f32[1024]{0:T(1024)S(1)} %fusion.114) | copy-start | bytes 12292
  383.8 195.7 %all-reduce.12.cloned.1.call-start = ((), (), s32[]{:S(2)}) async-start(), calls=%async_computation.13 | async-start | bytes 8388608 | tf_op jit(solution)/shard_map/psum | solution.py:65
  473.7 1.6 copy-start.5
  477.9 3.2 copy-start.35
  477.9 3.2 copy-start.37
  477.9 6.3 copy-start.38
  481.0 7.0 copy-start.4
  481.0 98.5 %copy-start.24 = (f32[1024]{0:T(1024)}, f32[1024]{0:T(1024)S(1)}, u32[]{:S(2)}) copy-start(f32[1024]{0:T(1024)S(1)} %negate_multiply_fusion.2) | copy-start | bytes 12292
  484.2 5.2 copy-start.34
  488.1 1.3 copy-start.40
  493.8 529.4 %reduce-scatter.15.cloned.1.call-start = ((), (), s32[]{:S(2)}) async-start(), calls=%async_computation.15 | async-start | bytes 5242880 | tf_op jit(solution)/shard_map/reduce_scatter | solution.py:213
  579.5 6.4 copy-start.1
  587.7 2.0 copy-start.3
  587.7 7.9 copy-start.22
  589.7 5.9 copy-start.2
  946.2 156.7 %reduce-scatter.13.cloned.1.call-start = ((), (), s32[]{:S(2)}) async-start(), calls=%async_computation.14 | async-start | bytes 5242880 | tf_op jit(solution)/shard_map/reduce_scatter | solution.py:210
  951.8 1.2 copy-start.7
  951.8 1.2 copy-start.23
  951.9 5.4 copy-start.25
  951.9 5.4 copy-start.39
  951.9 174.5 %reduce-scatter.19.cloned.1.call-start = ((), (), s32[]{:S(2)}) async-start(), calls=%async_computation.18 | async-start | bytes 1572864 | tf_op jit(solution)/shard_map/reduce_scatter | solution.py:231
  957.2 225.9 %reduce-scatter.23.cloned.1.call-start = ((), (), s32[]{:S(2)}) async-start(), calls=%async_computation.20 | async-start | bytes 6291456 | tf_op jit(solution)/shard_map/reduce_scatter | solution.py:233
  963.9 0.7 copy-start.17
  963.9 0.7 copy-start.19
  963.9 0.7 copy-start.21
  963.9 0.7 copy-start.28
  963.9 1.6 copy-start.41
  963.9 275.7 %reduce-scatter.21.cloned.1.call-start = ((), (), s32[]{:S(2)}) async-start(), calls=%async_computation.19 | async-start | bytes 6291456 | tf_op jit(solution)/shard_map/reduce_scatter | solution.py:232
  972.3 132.6 %copy-start.9 = (bf16[1024,1024]{1,0:T(8,128)(2,1)S(1)}, bf16[1024,1024]{1,0:T(8,128)(2,1)}, u32[]{:S(2)}) copy-start(bf16[1024,1024]{1,0:T(8,128)(2,1)} %param.13) | copy-start | bytes 6291460
  972.3 313.0 %reduce-scatter.17.cloned.1.call-start = ((), (), s32[]{:S(2)}) async-start(), calls=%async_computation.17 | async-start | bytes 4718592 | tf_op jit(solution)/shard_map/reduce_scatter | solution.py:230
  1104.1 0.8 copy-start.13
  1104.9 4.6 copy-start.29
  1104.9 4.6 copy-start.31
  1109.4 1.2 copy-start.26
  1109.4 1.2 copy-start.30
  1109.4 2.4 copy-start.12
  1109.5 2.4 copy-start.14
  1109.5 193.1 %reduce-scatter.27.cloned.1.call-start = ((), (), s32[]{:S(2)}) async-start(), calls=%async_computation.23 | async-start | bytes 786432
  1110.6 209.3 %reduce-scatter.25.cloned.1.call-start = ((), (), s32[]{:S(2)}) async-start(), calls=%async_computation.22 | async-start | bytes 786432
  1111.8 296.0 %all-reduce.14.cloned.1.call-start = ((), (), s32[]{:S(2)}) async-start(), calls=%async_computation.16 | async-start | bytes 8388608 | tf_op jit(solution)/shard_map/psum | solution.py:65
  1117.1 517.2 %all-reduce.16.cloned.1.call-start = ((), (), s32[]{:S(2)}) async-start(), calls=%async_computation.24 | async-start | bytes 12582912 | tf_op jit(solution)/shard_map/psum | solution.py:237
  1634.3 8.2 copy-start.11
Sparse Core Ops, SparseCore 0:
  10.1 29.8 all-gather.5
  45.2 72.1 all-gather.11
  222.6 85.2 all-reduce.7
  309.4 33.2 all-gather.7
  344.1 33.1 all-gather.9
  383.9 85.4 all-reduce.9
  493.9 85.6 all-reduce.11
  946.3 76.8 reduce-scatter.14
  1025.5 77.2 reduce-scatter.12
  1105.6 20.8 reduce-scatter.18
  1128.7 54.3 reduce-scatter.22
  1185.3 54.2 reduce-scatter.20
  1241.9 43.3 reduce-scatter.16
  1288.0 14.5 reduce-scatter.26
  1305.3 14.5 reduce-scatter.24
  1322.2 85.4 all-reduce.13
  1410.2 223.9 all-reduce.15
